TPU v7x, 512 devices: a whole 4x4x16 slice. The times are simulated.
512 devices in a mesh: shot: 16 (over z_hi, y), slab: 32 (over z_lo, x, core).
Axes of the slice: x: 4, y: 4, z: 16 (z_hi: 4, z_lo: 4; z = z_hi * 4 + z_lo), core: 2. Of those that a mesh axis runs over, the one named last changes fastest.
Arguments:
- wave_now: float32 [16, 512, 64, 128], P('shot', 'slab'), may hold values from -6 to 6
- wave_prev: float32 [16, 512, 64, 128], P('shot', 'slab'), may hold values from -6 to 6
- courant: float32 [512, 64, 128], P('slab'), may hold values from 0.05 to 0.2
- forward: bfloat16 [16, 3, 512, 64, 128], P('shot', None, 'slab'), may hold values from -6 to 6
- receivers: int32 [16, 3, 256], P('shot'), may hold values from 0 to 511, as said below
- residual: float32 [16, 3, 256], P('shot'), may hold values from -6 to 6
- aperture: int32 [16, 2], P('shot'), may hold values from 0 to 512, as said below
- latent: bfloat16 [256, 32, 4096], P('slab', 'shot')
- weight: float32 [64, 8], replicated, may hold values from -0.75 to 0.75
Outputs:
- wave_after: float32 [16, 512, 64, 128], P('shot', 'slab')
- wave_before: float32 [16, 512, 64, 128], P('shot', 'slab')
- latent_grad: float32 [256, 32, 4096], P('slab', 'shot')
- weight_grad: float32 [64, 8], replicated
Inputs may be any that keep to these rules, and one draw needn't show every extreme that they name: receivers[s,0,r], receivers[s,1,r], receivers[s,2,r] are an x, y and depth cell inside the grid. Each shot's aperture is a range of at least 512 // 4 x cells with aperture[s,0] < aperture[s,1].
All inputs are finite; a program needn't handle non-finite values.
Results may differ from a plain program's by a relative error of at most 0.0003.
Values sent between devices are 32-bit elements; how exact they have to be, the bound alone decides.
No kernel may reach another device: no remote copies, remote signals or barrier semaphores. Data moves between devices by JAX's collectives and lax.ppermute only.
A program may use at most 64 MiB of HBM per device.

v0:
```python
import math
import jax
import jax.numpy as jnp
from jax import lax
from jax.sharding import PartitionSpec as P

STEPS = 3
stencil_weights = (-205.0 / 72.0, 8.0 / 5.0, -1.0 / 5.0, 8.0 / 315.0, -1.0 / 560.0)


def extended(block, sides, width):
    for axis, dim in sides:
        count = lax.axis_size(axis)
        forward = [(i, i + 1) for i in range(count - 1)]
        backward = [(target, source) for source, target in forward]
        low = lax.ppermute(
            lax.slice_in_dim(block, block.shape[dim] - width, None, axis=dim), axis, forward
        )
        high = lax.ppermute(lax.slice_in_dim(block, 0, width, axis=dim), axis, backward)
        block = jnp.concatenate([low, block, high], axis=dim)
    return block


def laplace(padded):
    size_x = padded.shape[0] - 8
    size_y = padded.shape[1] - 8
    size_z = padded.shape[2] - 8

    def moved(shift_x, shift_y, shift_z):
        return padded[
            4 + shift_x : 4 + shift_x + size_x,
            4 + shift_y : 4 + shift_y + size_y,
            4 + shift_z : 4 + shift_z + size_z,
        ]

    total = 3.0 * stencil_weights[0] * moved(0, 0, 0)
    for offset in range(1, 5):
        cycle_sum = moved(offset, 0, 0) + moved(-offset, 0, 0)
        cycle_sum = cycle_sum + moved(0, offset, 0) + moved(0, -offset, 0)
        cycle_sum = cycle_sum + moved(0, 0, offset) + moved(0, 0, -offset)
        total = total + stencil_weights[offset] * cycle_sum
    return total


def pad_sides(field):
    return jnp.pad(field, ((0, 0), (4, 4), (4, 4)))


def inject(field, receivers, values, first_x):
    extent = field.shape[0]
    local_x = receivers[0, 0] - first_x
    valid = (local_x >= 0) & (local_x < extent)
    local_x = jnp.where(valid, local_x, extent)
    return field.at[local_x, receivers[0, 1], receivers[0, 2]].add(values, mode="drop")


def body(wave_now, wave_prev, courant, forward, receivers, residual, aperture, latent, weight):
    slab_cells = courant.shape[0]
    first_x = lax.axis_index("slab") * slab_cells
    current = wave_now[0]
    previous = wave_prev[0]
    accum = jnp.zeros(current.shape, jnp.float32)
    for instant in range(STEPS):
        padded = extended(current, (("slab", 0),), 4)
        advanced = 2.0 * current - previous + courant * laplace(pad_sides(padded))
        advanced = inject(advanced, receivers, residual[0, instant], first_x)
        accum = accum + advanced * forward[0, instant].astype(jnp.float32)
        previous = current
        current = advanced
    x_cells = first_x + jnp.arange(slab_cells, dtype=jnp.int32)
    inside = (x_cells >= aperture[0, 0]) & (x_cells < aperture[0, 1])
    image = jnp.where(inside[:, None, None], courant * accum, 0.0)
    image_rows = image.transpose(1, 0, 2)
    tile_rows = image_rows.shape[0] // lax.axis_size("shot")
    tile = lax.psum_scatter(image_rows, "shot", scatter_dimension=0, tiled=True).transpose(1, 0, 2)
    half_x = slab_cells // 2
    half_y = tile_rows // 2
    half_z = tile.shape[2] // 2
    taps = (
        tile.reshape(half_x, 2, half_y, 2, half_z, 2)
        .transpose(0, 2, 4, 1, 3, 5)
        .reshape(half_x, half_y, half_z, 8)
    )
    channels = weight.shape[0]
    latent_grad = jnp.einsum(
        "ijkq,cq->ijck", taps, weight, precision=lax.Precision.HIGHEST
    ).reshape(half_x, half_y, channels * half_z)
    latent_wide = latent.astype(jnp.float32).reshape(half_x, half_y, channels, half_z)
    partial_grad = jnp.einsum("ijck,ijkq->cq", latent_wide, taps, precision=lax.Precision.HIGHEST)
    latent_cells = (
        latent.shape[0] * lax.axis_size("slab") * latent.shape[1] * lax.axis_size("shot") * half_z
    )
    weight_grad = lax.psum(partial_grad, ("shot", "slab")) * (1.0 / math.sqrt(latent_cells))
    return (current[None], previous[None], latent_grad, weight_grad)


def solution(mesh):
    return jax.shard_map(
        body,
        mesh=mesh,
        in_specs=(
            P("shot", "slab", None, None),
            P("shot", "slab", None, None),
            P("slab", None, None),
            P("shot", None, "slab", None, None),
            P("shot", None, None),
            P("shot", None, None),
            P("shot", None),
            P("slab", "shot", None),
            P(),
        ),
        out_specs=(
            P("shot", "slab", None, None),
            P("shot", "slab", None, None),
            P("slab", "shot", None),
            P(),
        ),
        check_vma=False,
    )
```

profile of v0, /device:TPU:1, one launch (start us, length us, event | category | flops | bytes accessed | tf_op | source)
XLA Modules:
  0.0 334.7 jit_solution(5647150959445888792)
XLA Ops:
  7.2 1.1 slice_bitcast_fusion.1
  8.3 8.8 %collective-permute-start = (f32[4,64,128]{2,1,0:T(8,128)S(1)}, f32[4,64,128]{2,1,0:T(8,128)S(1)}, u32[]{:S(2)}, u32[]{:S(2)}) collective-permute-start(f32[4,64,128]{2,1,0:T(8,128)S(1)} %get-tuple-element.24), channel_id=1, source_target_pairs={{1,0},{2,1},{3,2},{4,3},{5,4},{6,5},{7,6},{8,7},{9,8},{10,9},{11,1... | collective-permute-start | bytes 393224 | tf_op jit(solution)/shard_map/ppermute | solution.py:19
  17.1 1.9 collective-permute-start.1
  19.0 0.7 fusion.67
  19.8 0.7 or_select_fusion
  20.5 0.5 collective-permute-done.1
  21.0 0.7 copy-done.6
  21.6 1.6 select_maximum_fusion.4
  23.2 3.7 %fusion.13 = f32[16,64,128]{2,1,0:T(8,128)S(1)} fusion(f32[16,64,128]{2,1,0:T(8,128)S(1)} %copy-done.3, f32[16,64,128]{2,1,0:T(8,128)S(1)} %bitcast.63, f32[4,64,128]{2,1,0:T(8,128)} %copy-done.6, f32[4,64,128]{2,1,0:T(8,128)S(1)} %collective-permute-done, f32[24,72,136]{2,1,0:T(8,128)S(1)} %select_maximum_fusion.4, f32[1,16,64,128]{3,2,1,0:T(8,128)} %param.10), kind=kLoop, calls=%fused_computation.40 | loop fusion | flops 5373952 | bytes 10747904 | tf_op jit(solution)/shard_map/add | solution.py:65
  26.9 15.6 %scatter_fusion = f32[16,64,128]{2,1,0:T(8,128)S(1)} fusion(f32[16,64,128]{2,1,0:T(8,128)S(1)} %fusion.13, s32[256]{0:T(256)S(1)} %bitcast.56, f32[256]{0:T(256)S(1)} %bitcast.69), kind=kCustom, calls=%fused_computation | custom fusion | flops 256 | bytes 6144 | tf_op jit(solution)/shard_map/scatter-add | solution.py:54
  42.5 4.3 %collective-permute-start.3 = (f32[4,64,128]{2,1,0:T(8,128)S(1)}, f32[4,64,128]{2,1,0:T(8,128)S(1)}, u32[]{:S(2)}, u32[]{:S(2)}) collective-permute-start(f32[4,64,128]{2,1,0:T(8,128)S(1)} %get-tuple-element.22), channel_id=1, source_target_pairs={{0,1},{1,2},{2,3},{3,4},{4,5},{5,6},{6,7},{7,8},{8,9},{9,10},{10,1... | collective-permute-start | bytes 393224 | tf_op jit(solution)/shard_map/ppermute | solution.py:16
  46.8 1.9 collective-permute-start.2
  48.9 4.2 %collective-permute-done.2 = f32[4,64,128]{2,1,0:T(8,128)S(1)} collective-permute-done((f32[4,64,128]{2,1,0:T(8,128)S(1)}, f32[4,64,128]{2,1,0:T(8,128)S(1)}, u32[]{:S(2)}, u32[]{:S(2)}) %collective-permute-start.2) | collective-permute-done | bytes 131104 | tf_op jit(solution)/shard_map/ppermute | solution.py:19
  53.1 0.5 select_maximum_fusion.2
  53.7 2.1 fusion.46
  55.8 15.6 %scatter_fusion.1 = f32[16,64,128]{2,1,0:T(8,128)S(1)} fusion(f32[16,64,128]{2,1,0:T(8,128)S(1)} %fusion.46, s32[256]{0:T(256)S(1)} %bitcast.57, f32[256]{0:T(256)S(1)} %bitcast.68), kind=kCustom, calls=%fused_computation.1 | custom fusion | flops 256 | bytes 6144 | tf_op jit(solution)/shard_map/scatter-add | solution.py:54
  71.4 1.9 collective-permute-start.5
  73.3 0.6 fusion.68
  73.9 1.3 compare_and_fusion
  75.2 2.6 collective-permute-start.4
  78.0 3.5 %collective-permute-done.4 = f32[4,64,128]{2,1,0:T(8,128)S(1)} collective-permute-done((f32[4,64,128]{2,1,0:T(8,128)S(1)}, f32[4,64,128]{2,1,0:T(8,128)S(1)}, u32[]{:S(2)}, u32[]{:S(2)}) %collective-permute-start.4) | collective-permute-done | bytes 131104 | tf_op jit(solution)/shard_map/ppermute | solution.py:19
  81.5 0.5 select_maximum_fusion
  82.1 2.1 fusion.36
  84.2 15.6 %scatter_fusion.2 = f32[16,64,128]{2,1,0:T(8,128)S(1)} fusion(f32[16,64,128]{2,1,0:T(8,128)S(1)} %fusion.36, s32[256]{0:T(256)S(1)} %bitcast.58, f32[256]{0:T(256)S(1)} %bitcast.67), kind=kCustom, calls=%fused_computation.2 | custom fusion | flops 256 | bytes 6144 | tf_op jit(solution)/shard_map/scatter-add | solution.py:54
  100.1 1.1 copy.23
  101.4 118.1 %reduce-scatter.2.cloned.1.call-done = f32[4,16,128]{2,1,0:T(8,128)} async-done(((f32[64,16,128]{2,1,0:T(8,128)}), f32[4,16,128]{2,1,0:T(8,128)}) %reduce-scatter.2.cloned.1.call-update) | async-done | bytes 32784 | tf_op jit(solution)/shard_map/reduce_scatter | solution.py:75
  219.6 2.8 reshape.124
  222.4 0.7 copy.24
  223.1 1.0 convolution_bitcast_fusion
  224.3 1.0 reshape.151
  225.6 101.6 %psum.7 = f32[64,8]{0,1:T(8,128)S(1)} all-reduce(f32[64,8]{0,1:T(8,128)S(1)} %convolution_bitcast_fusion.1), channel_id=1, replica_groups=mesh['shot'=16,'slab'=32] {'shot','slab'}, use_global_device_ids=true, to_apply=%region_4.5 | all-reduce | flops 512 | bytes 4096 | tf_op jit(solution)/shard_map/psum | solution.py:93
  327.2 0.6 broadcast_multiply_fusion
  (34 shorter events, 1.4 us)
Async XLA Ops:
  7.2 215.9 %copy-start = (f32[64,8]{0,1:T(8,128)S(1)}, f32[64,8]{0,1:T(8,128)}, u32[]{:S(2)}) copy-start(f32[64,8]{0,1:T(8,128)} %param.17) | copy-start | bytes 6148
  7.2 16.0 %copy-start.4 = (f32[1,16,64,128]{3,2,1,0:T(8,128)S(1)}, f32[1,16,64,128]{3,2,1,0:T(8,128)}, u32[]{:S(2)}) copy-start(f32[1,16,64,128]{3,2,1,0:T(8,128)} %param.9) | copy-start | bytes 1572868
  7.2 16.0 %copy-start.3 = (f32[16,64,128]{2,1,0:T(8,128)S(1)}, f32[16,64,128]{2,1,0:T(8,128)}, u32[]{:S(2)}) copy-start(f32[16,64,128]{2,1,0:T(8,128)} %param.11) | copy-start | bytes 1572868
  7.2 212.3 %reduce-scatter.2.cloned.1.call-start = ((), (), s32[]{:S(2)}) async-start(), calls=%async_computation.1 | async-start | bytes 557056 | tf_op jit(solution)/shard_map/reduce_scatter | solution.py:75
  8.3 12.2 %collective-permute-start = (f32[4,64,128]{2,1,0:T(8,128)S(1)}, f32[4,64,128]{2,1,0:T(8,128)S(1)}, u32[]{:S(2)}, u32[]{:S(2)}) collective-permute-start(f32[4,64,128]{2,1,0:T(8,128)S(1)} %get-tuple-element.24), channel_id=1, source_target_pairs={{1,0},{2,1},{3,2},{4,3},{5,4},{6,5},{7,6},{8,7},{9,8},{10,9},{11,1... | collective-permute-start | bytes 393224 | tf_op jit(solution)/shard_map/ppermute | solution.py:19
  17.1 3.9 %collective-permute-start.1 = (f32[4,64,128]{2,1,0:T(8,128)S(1)}, f32[4,64,128]{2,1,0:T(8,128)S(1)}, u32[]{:S(2)}, u32[]{:S(2)}) collective-permute-start(f32[4,64,128]{2,1,0:T(8,128)S(1)} %get-tuple-element.25), channel_id=1, source_target_pairs={{0,1},{1,2},{2,3},{3,4},{4,5},{5,6},{6,7},{7,8},{8,9},{9,10},{10,1... | collective-permute-start | bytes 393224 | tf_op jit(solution)/shard_map/ppermute | solution.py:16
  21.0 0.7 copy-start.6
  42.5 6.3 %collective-permute-start.3 = (f32[4,64,128]{2,1,0:T(8,128)S(1)}, f32[4,64,128]{2,1,0:T(8,128)S(1)}, u32[]{:S(2)}, u32[]{:S(2)}) collective-permute-start(f32[4,64,128]{2,1,0:T(8,128)S(1)} %get-tuple-element.22), channel_id=1, source_target_pairs={{0,1},{1,2},{2,3},{3,4},{4,5},{5,6},{6,7},{7,8},{8,9},{9,10},{10,1... | collective-permute-start | bytes 393224 | tf_op jit(solution)/shard_map/ppermute | solution.py:16
  46.8 6.3 %collective-permute-start.2 = (f32[4,64,128]{2,1,0:T(8,128)S(1)}, f32[4,64,128]{2,1,0:T(8,128)S(1)}, u32[]{:S(2)}, u32[]{:S(2)}) collective-permute-start(f32[4,64,128]{2,1,0:T(8,128)S(1)} %get-tuple-element.23), channel_id=1, source_target_pairs={{1,0},{2,1},{3,2},{4,3},{5,4},{6,5},{7,6},{8,7},{9,8},{10,9},{11,1... | collective-permute-start | bytes 393224 | tf_op jit(solution)/shard_map/ppermute | solution.py:19
  55.8 17.5 %copy-start.8 = (s32[1,2]{1,0:T(1,128)S(1)}, s32[1,2]{1,0:T(1,128)}, u32[]{:S(2)}) copy-start(s32[1,2]{1,0:T(1,128)} %param.15) | copy-start | bytes 28
  71.4 28.4 %copy-start.1 = (f32[16,64,128]{2,1,0:T(8,128)}, f32[16,64,128]{2,1,0:T(8,128)S(1)}, u32[]{:S(2)}) copy-start(f32[16,64,128]{2,1,0:T(8,128)S(1)} %scatter_fusion.1) | copy-start | bytes 1572868
  71.4 6.4 %collective-permute-start.5 = (f32[4,64,128]{2,1,0:T(8,128)S(1)}, f32[4,64,128]{2,1,0:T(8,128)S(1)}, u32[]{:S(2)}, u32[]{:S(2)}) collective-permute-start(f32[4,64,128]{2,1,0:T(8,128)S(1)} %get-tuple-element.18), channel_id=1, source_target_pairs={{0,1},{1,2},{2,3},{3,4},{4,5},{5,6},{6,7},{7,8},{8,9},{9,10},{10,1... | collective-permute-start | bytes 393224 | tf_op jit(solution)/shard_map/ppermute | solution.py:16
  75.2 6.3 %collective-permute-start.4 = (f32[4,64,128]{2,1,0:T(8,128)S(1)}, f32[4,64,128]{2,1,0:T(8,128)S(1)}, u32[]{:S(2)}, u32[]{:S(2)}) collective-permute-start(f32[4,64,128]{2,1,0:T(8,128)S(1)} %get-tuple-element.19), channel_id=1, source_target_pairs={{1,0},{2,1},{3,2},{4,3},{5,4},{6,5},{7,6},{8,7},{9,8},{10,9},{11,1... | collective-permute-start | bytes 393224 | tf_op jit(solution)/shard_map/ppermute | solution.py:19
  84.2 15.6 %copy-start.5 = (bf16[1,3,16,64,128]{4,3,2,1,0:T(8,128)(2,1)S(1)}, bf16[1,3,16,64,128]{4,3,2,1,0:T(8,128)(2,1)}, u32[]{:S(2)}) copy-start(bf16[1,3,16,64,128]{4,3,2,1,0:T(8,128)(2,1)} %param.12) | copy-start | bytes 2359300
  99.8 1.4 copy-start.2
  99.8 1.4 copy-start.7
Sparse Core Ops, SparseCore 0:
  101.3 118.1 reduce-scatter.1
where the time goes:
time: 335 us
  waiting for transfers between devices  126 us (38%)
  blocking collectives  102 us (30%)
  other arithmetic  60 us (18%)
  starting transfers between devices  21.5 us (6%)
  between operations  14.4 us (4%)
  local copies, waits for them, and re-layouts  9.37 us (3%)
    reduce_scatter x1, waiting for transfers between devices, body(): lax.psum_scatter(image_rows, 'shot', scatter_dimension=0, tiled=True)  118 us
    psum x1, blocking collectives, body(): lax.psum(partial_grad, ('shot', 'slab')) * (1.0 / math.sqrt(latent_cells))  102 us
    scatter-add x3, other arithmetic, inject(): field.at[local_x, receivers[0, 1], receivers[0, 2]].add(values, mode='drop')  46.7 us
    ppermute x3, starting transfers between devices, extended(): lax.ppermute(lax.slice_in_dim(block, 0, width, axis=dim), axis, backward)  13.3 us
    ppermute x3, starting transfers between devices, extended(): lax.ppermute(lax.slice_in_dim(block, block.shape[dim] - width, None, axis...  8.19 us
    add x3, other arithmetic, body(): advanced = 2.0 * current - previous + courant * laplace(pad_sides(padded))  7.87 us
    ppermute x3, waiting for transfers between devices, extended(): lax.ppermute(lax.slice_in_dim(block, 0, width, axis=dim), axis, backward)  7.76 us
  transfers between devices with their start and end apart: 7, of which 4 were waited for; matrix products, arithmetic and copies ran while one was open for 1% of the time, Pallas kernels for 0%

commit v1 on v0

--- a/solution.py
+++ b/solution.py
@@ -90,7 +90,9 @@
     latent_cells = (
         latent.shape[0] * lax.axis_size("slab") * latent.shape[1] * lax.axis_size("shot") * half_z
     )
-    weight_grad = lax.psum(partial_grad, ("shot", "slab")) * (1.0 / math.sqrt(latent_cells))
+    weight_grad = jnp.sum(lax.all_gather(partial_grad, ("shot", "slab")), axis=0) * (
+        1.0 / math.sqrt(latent_cells)
+    )
     return (current[None], previous[None], latent_grad, weight_grad)
 
 

time: 335 us -> 993 us (2.96)
  waiting for transfers between devices: 126 us -> 883 us
  blocking collectives: 102 us -> 0 us
    all_gather x0 -> x1, waiting for transfers between devices: none -> 757 us  [body(): lax.all_gather(partial_grad, ('shot', 'slab'))]
    psum x1 -> x0, blocking collectives: 102 us -> none  [body(): lax.psum(partial_grad, ('shot', 'slab')) * (1.0 / math.sqrt(latent_cells))]
  transfers between devices with their start and end apart: 7 -> 8, of which waited for: 4 -> 5; matrix products, arithmetic and copies ran while one was open for 1% -> 1% of each run, Pallas kernels for 0% -> 0%
where the time goes in v1:
time: 993 us
  waiting for transfers between devices  883 us (89%)
  other arithmetic  62.2 us (6%)
  starting transfers between devices  21.6 us (2%)
  between operations  14.4 us (1%)
    all_gather x1, waiting for transfers between devices, body(): lax.all_gather(partial_grad, ('shot', 'slab'))  757 us
    reduce_scatter x1, waiting for transfers between devices, body(): lax.psum_scatter(image_rows, 'shot', scatter_dimension=0, tiled=True)  118 us
    scatter-add x3, other arithmetic, inject(): field.at[local_x, receivers[0, 1], receivers[0, 2]].add(values, mode='drop')  46.7 us
  transfers between devices with their start and end apart: 8, of which 5 were waited for; matrix products, arithmetic and copies ran while one was open for 1% of the time, Pallas kernels for 0%

profile of v1, /device:TPU:1, one launch (start us, length us, event | category | flops | bytes accessed | tf_op | source)
XLA Modules:
  0.0 992.7 jit_solution(2116766139591605811)
XLA Ops:
  7.2 1.1 slice_bitcast_fusion.1
  8.3 8.8 collective-permute-start
  17.1 1.9 collective-permute-start.1
  19.0 0.7 fusion.67
  19.8 0.7 or_select_fusion
  21.0 0.7 copy-done.6
  21.6 1.6 select_maximum_fusion.4
  23.2 3.7 fusion.13
  26.9 15.6 %scatter_fusion = f32[16,64,128]{2,1,0:T(8,128)S(1)} fusion(f32[16,64,128]{2,1,0:T(8,128)S(1)} %fusion.13, s32[256]{0:T(256)S(1)} %bitcast.58, f32[256]{0:T(256)S(1)} %bitcast.71), kind=kCustom, calls=%fused_computation | custom fusion | flops 256 | bytes 6144 | tf_op jit(solution)/shard_map/scatter-add | solution.py:54
  42.5 4.3 collective-permute-start.3
  46.9 1.9 collective-permute-start.2
  48.9 4.2 collective-permute-done.2
  53.1 0.5 select_maximum_fusion.2
  53.7 2.1 fusion.46
  55.8 15.6 %scatter_fusion.1 = f32[16,64,128]{2,1,0:T(8,128)S(1)} fusion(f32[16,64,128]{2,1,0:T(8,128)S(1)} %fusion.46, s32[256]{0:T(256)S(1)} %bitcast.59, f32[256]{0:T(256)S(1)} %bitcast.70), kind=kCustom, calls=%fused_computation.1 | custom fusion | flops 256 | bytes 6144 | tf_op jit(solution)/shard_map/scatter-add | solution.py:54
  71.4 1.9 collective-permute-start.5
  73.3 0.6 fusion.68
  73.9 1.3 compare_and_fusion
  75.2 2.4 collective-permute-start.4
  77.8 3.7 collective-permute-done.4
  82.1 2.1 fusion.36
  84.2 15.6 %scatter_fusion.2 = f32[16,64,128]{2,1,0:T(8,128)S(1)} fusion(f32[16,64,128]{2,1,0:T(8,128)S(1)} %fusion.36, s32[256]{0:T(256)S(1)} %bitcast.60, f32[256]{0:T(256)S(1)} %bitcast.69), kind=kCustom, calls=%fused_computation.2 | custom fusion | flops 256 | bytes 6144 | tf_op jit(solution)/shard_map/scatter-add | solution.py:54
  100.1 1.1 copy.23
  101.7 117.9 %reduce-scatter.2.cloned.1.call-done = f32[4,16,128]{2,1,0:T(8,128)} async-done(((f32[64,16,128]{2,1,0:T(8,128)}), f32[4,16,128]{2,1,0:T(8,128)}) %reduce-scatter.2.cloned.1.call-update) | async-done | bytes 32784 | tf_op jit(solution)/shard_map/reduce_scatter | solution.py:75
  219.6 2.8 reshape.124
  222.4 0.7 copy.24
  223.1 0.9 convolution_bitcast_fusion.1
  224.1 1.0 convolution_bitcast_fusion
  225.3 1.0 reshape.155
  226.3 756.9 %all-gather.4.cloned.1.call-done = f32[512,64,8]{1,2,0:T(8,128)} async-done(((f32[1,64,8]{1,2,0:T(8,128)}), f32[512,64,8]{1,2,0:T(8,128)}) %all-gather.4.cloned.1.call-update) | async-done | bytes 1048592 | tf_op jit(solution)/shard_map/all_gather | solution.py:93
  983.2 2.1 reduce_sum.9
  985.3 0.6 broadcast_multiply_fusion
  (37 shorter events, 2.3 us)
Async XLA Ops:
  7.2 216.9 %copy-start = (f32[64,8]{0,1:T(8,128)S(1)}, f32[64,8]{0,1:T(8,128)}, u32[]{:S(2)}) copy-start(f32[64,8]{0,1:T(8,128)} %param.17) | copy-start | bytes 6148
  7.2 16.0 %copy-start.4 = (f32[1,16,64,128]{3,2,1,0:T(8,128)S(1)}, f32[1,16,64,128]{3,2,1,0:T(8,128)}, u32[]{:S(2)}) copy-start(f32[1,16,64,128]{3,2,1,0:T(8,128)} %param.9) | copy-start | bytes 1572868
  7.2 16.0 %copy-start.3 = (f32[16,64,128]{2,1,0:T(8,128)S(1)}, f32[16,64,128]{2,1,0:T(8,128)}, u32[]{:S(2)}) copy-start(f32[16,64,128]{2,1,0:T(8,128)} %param.11) | copy-start | bytes 1572868
  7.2 212.4 %reduce-scatter.2.cloned.1.call-start = ((), (), s32[]{:S(2)}) async-start(), calls=%async_computation.1 | async-start | bytes 557056 | tf_op jit(solution)/shard_map/reduce_scatter | solution.py:75
  8.3 12.2 %collective-permute-start = (f32[4,64,128]{2,1,0:T(8,128)S(1)}, f32[4,64,128]{2,1,0:T(8,128)S(1)}, u32[]{:S(2)}, u32[]{:S(2)}) collective-permute-start(f32[4,64,128]{2,1,0:T(8,128)S(1)} %get-tuple-element.24), channel_id=1, source_target_pairs={{1,0},{2,1},{3,2},{4,3},{5,4},{6,5},{7,6},{8,7},{9,8},{10,9},{11,1... | collective-permute-start | bytes 393224 | tf_op jit(solution)/shard_map/ppermute | solution.py:19
  17.1 3.9 collective-permute-start.1
  21.0 0.7 copy-start.6
  42.5 6.3 collective-permute-start.3
  46.9 6.3 collective-permute-start.2
  55.8 17.5 %copy-start.8 = (s32[1,2]{1,0:T(1,128)S(1)}, s32[1,2]{1,0:T(1,128)}, u32[]{:S(2)}) copy-start(s32[1,2]{1,0:T(1,128)} %param.15) | copy-start | bytes 28
  71.4 28.4 %copy-start.1 = (f32[16,64,128]{2,1,0:T(8,128)}, f32[16,64,128]{2,1,0:T(8,128)S(1)}, u32[]{:S(2)}) copy-start(f32[16,64,128]{2,1,0:T(8,128)S(1)} %scatter_fusion.1) | copy-start | bytes 1572868
  71.4 6.2 collective-permute-start.5
  75.2 6.3 collective-permute-start.4
  84.2 15.6 %copy-start.5 = (bf16[1,3,16,64,128]{4,3,2,1,0:T(8,128)(2,1)S(1)}, bf16[1,3,16,64,128]{4,3,2,1,0:T(8,128)(2,1)}, u32[]{:S(2)}) copy-start(bf16[1,3,16,64,128]{4,3,2,1,0:T(8,128)(2,1)} %param.12) | copy-start | bytes 2359300
  99.8 1.4 copy-start.2
  99.8 1.7 copy-start.7
  101.2 881.9 %all-gather.4.cloned.1.call-start = ((), (), s32[]{:S(2)}) async-start(), calls=%async_computation.2 | async-start | bytes 2101248 | tf_op jit(solution)/shard_map/all_gather | solution.py:93
Sparse Core Ops, SparseCore 0:
  101.3 118.1 reduce-scatter.1
  224.2 758.9 all-gather.3
